TPU v7x, 32 devices: a whole 2x2x4 slice. The times are simulated.
32 devices in a mesh: dp: 8 (over y, x, core), head: 4 (over z).
Axes of the slice: x: 2, y: 2, z: 4, core: 2. Of those that a mesh axis runs over, the one named last changes fastest.
Arguments:
- tokens: bfloat16 [16384, 1024], P(('dp', 'head')), may hold values from -6 to 6
- first_values: bfloat16 [16384, 1024], P('dp', 'head'), may hold values from -6 to 6
- mixer_in: float32 [3, 1024, 1024], P(None, 'dp', 'head'), may hold values from -0.1875 to 0.1875
- mixer_out: float32 [1024, 1024], P('head', 'dp'), may hold values from -0.75 to 0.75
- gate_up: float32 [2, 1024, 2816], P(None, 'dp', 'head'), may hold values from -0.1875 to 0.1875
- down_weight: float32 [2816, 1024], P('head', 'dp'), may hold values from -0.109375 to 0.109375
- norm_gains: float32 [2, 1024], P(None, 'dp'), may hold values from 0.5 to 1.5
- lengths: int32 [8], P('dp'), may hold values from 128 to 2048, as said below
- cotangent: bfloat16 [16384, 1024], P(('dp', 'head')), may hold values from -6 to 6
Outputs:
- block_out: bfloat16 [16384, 1024], P(('dp', 'head'))
- tokens_grad: float32 [16384, 1024], P(('dp', 'head'))
- first_grad: float32 [16384, 1024], P('dp', 'head')
- mixer_in_grad: float32 [3, 1024, 1024], P(None, 'dp', 'head')
- mixer_out_grad: float32 [1024, 1024], P('head', 'dp')
- gate_up_grad: float32 [2, 1024, 2816], P(None, 'dp', 'head')
- down_grad: float32 [2816, 1024], P('head', 'dp')
- gains_grad: float32 [2, 1024], P(None, 'dp')
Inputs may be any that keep to these rules, and one draw needn't show every extreme that they name: `lengths`: positions from a sequence's length on are padding; some sequence has exactly 2048 real tokens in every draw.
All inputs are finite; a program needn't handle non-finite values.
Results may differ from a plain program's by a relative error of at most 0.013.
The roundings to bfloat16 on the way count: a program that leaves them out, or rounds other values in their place, can miss the bound.
Values may be sent and summed in bfloat16 or wider, within the bound.
No kernel may reach another device: no remote copies, remote signals or barrier semaphores. Data moves between devices by JAX's collectives and lax.ppermute only.
A program may use at most 128 MiB of HBM per device.

v0:
```python
import jax
import jax.numpy as jnp
from jax import lax
from jax.sharding import PartitionSpec as P

HDIM = 64
SEQ = 2048
epsilon = 1e-05
far_below = -1e30
rope_base = 10000.0


def rope_tables(width):
    half = width // 2
    rates = rope_base ** (-jnp.arange(half, dtype=jnp.float32) * 2.0 / width)
    angles = jnp.arange(SEQ, dtype=jnp.float32)[:, None] * rates[None, :]
    return (jnp.cos(angles)[:, None, :], jnp.sin(angles)[:, None, :])


def rotate(field, cosine, sine, direction):
    half = field.shape[-1] // 2
    first = field[..., :half]
    second = field[..., half:]
    return jnp.concatenate(
        [first * cosine - direction * second * sine, second * cosine + direction * first * sine],
        axis=-1,
    )


def rms_parts(field, gain):
    factor = lax.rsqrt(jnp.mean(field * field, axis=-1, keepdims=True) + epsilon)
    unit = field * factor
    return (unit * gain, unit, factor)


def rms_back(normed_grad, unit, factor, gain):
    scaled = normed_grad * gain
    field_grad = factor * (scaled - unit * jnp.mean(scaled * unit, axis=-1, keepdims=True))
    return (field_grad, jnp.sum(normed_grad * unit, axis=0))


def to_items(rows, seqs_here, heads_here):
    return (
        rows.reshape(seqs_here, SEQ, heads_here, HDIM)
        .transpose(0, 2, 1, 3)
        .reshape(seqs_here * heads_here, SEQ, HDIM)
    )


def from_items(items, seqs_here, heads_here):
    return (
        items.reshape(seqs_here, heads_here, SEQ, HDIM)
        .transpose(0, 2, 1, 3)
        .reshape(seqs_here * SEQ, heads_here * HDIM)
    )


def block_scores(query_block, keys, rows, length):
    places = jnp.arange(SEQ)
    raw = jnp.einsum("qe,ke->qk", query_block, keys, preferred_element_type=jnp.float32)
    allowed = (places[None, :] <= rows[:, None]) & (places[None, :] < length)
    return jnp.where(allowed, raw * HDIM ** (-0.5), far_below)


def attend_item(item):
    query, keys, values, length = item
    block = min(512, SEQ)

    def one_block(number):
        start = number * block
        query_block = lax.dynamic_slice_in_dim(query, start, block, 0)
        rows = start + jnp.arange(block)
        scores = block_scores(query_block, keys, rows, length)
        peak = jnp.max(scores, axis=-1, keepdims=True)
        powers = jnp.exp(scores - peak)
        total = jnp.sum(powers, axis=-1, keepdims=True)
        probs = (powers / total).astype(jnp.bfloat16)
        result = (
            jnp.dot(probs, values, preferred_element_type=jnp.float32) * (rows < length)[:, None]
        )
        return (result.astype(jnp.bfloat16), (peak + jnp.log(total))[:, 0])

    results, log_total = lax.map(one_block, jnp.arange(SEQ // block))
    return (results.reshape(SEQ, HDIM), log_total.reshape(SEQ))


def attend_back(item):
    query, keys, values, length, log_total, out_grad = item
    block = min(512, SEQ)

    def one_block(carry, number):
        keys_grad, values_grad = carry
        start = number * block
        query_block = lax.dynamic_slice_in_dim(query, start, block, 0)
        grad_block = lax.dynamic_slice_in_dim(out_grad, start, block, 0)
        total_block = lax.dynamic_slice_in_dim(log_total, start, block, 0)
        rows = start + jnp.arange(block)
        scores = block_scores(query_block, keys, rows, length)
        probs = jnp.exp(scores - total_block[:, None])
        values_grad = values_grad + jnp.einsum(
            "qk,qe->ke", probs.astype(jnp.bfloat16), grad_block, preferred_element_type=jnp.float32
        )
        prob_grad = jnp.einsum("qe,ke->qk", grad_block, values, preferred_element_type=jnp.float32)
        offset = jnp.sum(prob_grad * probs, axis=-1, keepdims=True)
        raw_grad = (probs * (prob_grad - offset) * HDIM ** (-0.5)).astype(jnp.bfloat16)
        query_grad = jnp.dot(raw_grad, keys, preferred_element_type=jnp.float32)
        keys_grad = keys_grad + jnp.einsum(
            "qk,qe->ke", raw_grad, query_block, preferred_element_type=jnp.float32
        )
        return ((keys_grad, values_grad), query_grad)

    empty = jnp.zeros((SEQ, HDIM), jnp.float32)
    (keys_grad, values_grad), query_grads = lax.scan(
        one_block, (empty, empty), jnp.arange(SEQ // block)
    )
    return (query_grads.reshape(SEQ, HDIM), keys_grad, values_grad)


def shards(
    tokens, first_values, mixer_in, mixer_out, gate_up, down_weight, norm_gains, lengths, cotangent
):
    seqs_here = lengths.shape[0]
    group_rows = seqs_here * SEQ
    heads_here = mixer_in.shape[2] // HDIM
    cosine, sine = rope_tables(HDIM)
    places = jnp.arange(SEQ)
    valid_rows = (places[None, :] < lengths[:, None]).astype(jnp.float32).reshape(group_rows)
    head_lengths = jnp.repeat(lengths, heads_here)
    qkv_low = mixer_in.astype(jnp.bfloat16)
    proj_low = mixer_out.astype(jnp.bfloat16)
    gates_low = gate_up.astype(jnp.bfloat16)
    down_low = down_weight.astype(jnp.bfloat16)
    gain_low = norm_gains.astype(jnp.bfloat16)
    full = (
        lax.all_gather(qkv_low, "dp", axis=1, tiled=True),
        lax.all_gather(proj_low, "dp", axis=1, tiled=True),
        lax.all_gather(gates_low, "dp", axis=1, tiled=True),
        lax.all_gather(down_low, "dp", axis=1, tiled=True),
        lax.all_gather(gain_low, "dp", axis=1, tiled=True),
    )
    qkv_full, proj_full, gates_full, down_full, gain_full = full
    gain_first = gain_full[0].astype(jnp.float32)
    gain_second = gain_full[1].astype(jnp.float32)
    token_rows = tokens.astype(jnp.float32)
    normed_a, unit_a, factor_a = rms_parts(token_rows, gain_first)
    mixer_rows = lax.all_gather(normed_a.astype(jnp.bfloat16), "head", axis=0, tiled=True)
    mixed = jnp.einsum("td,kdc->ktc", mixer_rows, qkv_full, preferred_element_type=jnp.float32)
    shape_four = (seqs_here, SEQ, heads_here, HDIM)
    query = rotate(mixed[0].reshape(shape_four), cosine, sine, 1.0).astype(jnp.bfloat16)
    keys = rotate(mixed[1].reshape(shape_four), cosine, sine, 1.0).astype(jnp.bfloat16)
    values = (0.5 * mixed[2] + 0.5 * first_values.astype(jnp.float32)).astype(jnp.bfloat16)
    query_items = query.transpose(0, 2, 1, 3).reshape(seqs_here * heads_here, SEQ, HDIM)
    keys_items = keys.transpose(0, 2, 1, 3).reshape(seqs_here * heads_here, SEQ, HDIM)
    values_items = to_items(values, seqs_here, heads_here)
    attended_items, log_total = lax.map(
        attend_item, (query_items, keys_items, values_items, head_lengths)
    )
    attended = from_items(attended_items, seqs_here, heads_here)
    piece = attended
    branch_a = lax.psum_scatter(
        jnp.dot(piece, proj_full, preferred_element_type=jnp.float32),
        "head",
        scatter_dimension=0,
        tiled=True,
    )
    hidden_state = token_rows + branch_a
    normed_b, unit_b, factor_b = rms_parts(hidden_state, gain_second)
    feed_rows = lax.all_gather(normed_b.astype(jnp.bfloat16), "head", axis=0, tiled=True)
    gated = jnp.einsum("td,kdf->ktf", feed_rows, gates_full, preferred_element_type=jnp.float32)
    gate = gated[0]
    upward = gated[1]
    sigmoid_gate = jax.nn.sigmoid(gate)
    silu_gate = gate * sigmoid_gate
    inner = (silu_gate * upward).astype(jnp.bfloat16)
    piece = inner
    branch_b = lax.psum_scatter(
        jnp.dot(piece, down_full, preferred_element_type=jnp.float32).astype(jnp.bfloat16),
        "head",
        scatter_dimension=0,
        tiled=True,
    ).astype(jnp.float32)
    block_out = (hidden_state + branch_b).astype(jnp.bfloat16)
    back_full = (
        lax.all_gather(qkv_low, "dp", axis=1, tiled=True),
        lax.all_gather(proj_low, "dp", axis=1, tiled=True),
        lax.all_gather(gates_low, "dp", axis=1, tiled=True),
        lax.all_gather(down_low, "dp", axis=1, tiled=True),
        lax.all_gather(gain_low, "dp", axis=1, tiled=True),
    )
    qkv_back, proj_back, gates_back, down_back, gain_back = back_full
    piece = lax.all_gather(cotangent, "head", axis=0, tiled=True)
    down_sum = jnp.einsum("tf,td->fd", inner, piece, preferred_element_type=jnp.float32)
    rows_grad = jnp.einsum("td,fd->tf", piece, down_back, preferred_element_type=jnp.float32)
    inner_grad = rows_grad
    gate_grad = inner_grad * upward * sigmoid_gate * (1.0 + gate * (1.0 - sigmoid_gate))
    mlp_grad = jnp.stack([gate_grad, inner_grad * silu_gate]).astype(jnp.bfloat16)
    gates_part = jnp.einsum("td,ktf->kdf", feed_rows, mlp_grad, preferred_element_type=jnp.float32)
    piece = mlp_grad
    normed_b_grad = lax.psum_scatter(
        jnp.einsum("ktf,kdf->td", piece, gates_back, preferred_element_type=jnp.float32),
        "head",
        scatter_dimension=0,
        tiled=True,
    )
    state_part, gain_b_grad = rms_back(
        normed_b_grad, unit_b, factor_b, gain_back[1].astype(jnp.float32)
    )
    state_grad = cotangent.astype(jnp.float32) + state_part
    branch_grad = state_grad.astype(jnp.bfloat16)
    piece = lax.all_gather(branch_grad, "head", axis=0, tiled=True)
    proj_sum = jnp.einsum("tc,td->cd", attended, piece, preferred_element_type=jnp.float32)
    rows_grad = jnp.einsum("td,cd->tc", piece, proj_back, preferred_element_type=jnp.float32)
    attended_grad = rows_grad
    attended_grad = (valid_rows[:, None] * attended_grad).astype(jnp.bfloat16)
    grad_items = to_items(attended_grad, seqs_here, heads_here)
    query_grad, keys_grad, values_grad = lax.map(
        attend_back, (query_items, keys_items, values_items, head_lengths, log_total, grad_items)
    )
    values_mix_grad = from_items(values_grad, seqs_here, heads_here)
    first_grad = 0.5 * values_mix_grad
    query_rows = query_grad.reshape(seqs_here, heads_here, SEQ, HDIM).transpose(0, 2, 1, 3)
    keys_rows = keys_grad.reshape(seqs_here, heads_here, SEQ, HDIM).transpose(0, 2, 1, 3)
    query_back = rotate(query_rows, cosine, sine, -1.0).reshape(group_rows, heads_here * HDIM)
    keys_back = rotate(keys_rows, cosine, sine, -1.0).reshape(group_rows, heads_here * HDIM)
    mixed_grad = jnp.stack([query_back, keys_back, 0.5 * values_mix_grad]).astype(jnp.bfloat16)
    qkv_part = jnp.einsum("td,ktc->kdc", mixer_rows, mixed_grad, preferred_element_type=jnp.float32)
    piece = mixed_grad
    normed_a_grad = lax.psum_scatter(
        jnp.einsum("ktc,kdc->td", piece, qkv_back, preferred_element_type=jnp.float32).astype(
            jnp.bfloat16
        ),
        "head",
        scatter_dimension=0,
        tiled=True,
    ).astype(jnp.float32)
    token_part, gain_a_grad = rms_back(
        normed_a_grad, unit_a, factor_a, gain_back[0].astype(jnp.float32)
    )
    tokens_grad = state_grad + token_part
    gain_grads = jnp.stack([gain_a_grad, gain_b_grad])
    summed = (
        lax.psum_scatter(qkv_part, "dp", scatter_dimension=1, tiled=True),
        lax.psum_scatter(proj_sum, "dp", scatter_dimension=1, tiled=True),
        lax.psum_scatter(gates_part, "dp", scatter_dimension=1, tiled=True),
        lax.psum_scatter(down_sum, "dp", scatter_dimension=1, tiled=True),
        lax.psum_scatter(gain_grads, "dp", scatter_dimension=1, tiled=True),
    )
    gains_grad = lax.psum(summed[4], "head")
    return (
        block_out,
        tokens_grad,
        first_grad,
        summed[0],
        summed[1],
        summed[2],
        summed[3],
        gains_grad,
    )


def solution(mesh):
    return jax.shard_map(
        shards,
        mesh=mesh,
        in_specs=(
            P(("dp", "head"), None),
            P("dp", "head"),
            P(None, "dp", "head"),
            P("head", "dp"),
            P(None, "dp", "head"),
            P("head", "dp"),
            P(None, "dp"),
            P("dp"),
            P(("dp", "head"), None),
        ),
        out_specs=(
            P(("dp", "head"), None),
            P(("dp", "head"), None),
            P("dp", "head"),
            P(None, "dp", "head"),
            P("head", "dp"),
            P(None, "dp", "head"),
            P("head", "dp"),
            P(None, "dp"),
        ),
        check_vma=False,
    )
```

profile of v0, /device:TPU:0, one launch (start us, length us, event | category | flops | bytes accessed | tf_op | source)
XLA Modules:
  0.0 1471.1 jit_solution(9712456741320512277)
XLA Ops:
  7.2 1.9 copy.60
  9.9 10.2 all_gather.32
  25.0 12.0 all_gather.35
  39.8 83.2 %all-gather.8.cloned.1.call-done = bf16[2048,1024]{1,0:T(8,128)(2,1)} async-done(((bf16[512,1024]{1,0:T(8,128)(2,1)}), bf16[2048,1024]{1,0:T(8,128)(2,1)}) %all-gather.8.cloned.1.call-update) | async-done | bytes 4194320 | tf_op jit(solution)/shard_map/all_gather | solution.py:146
  123.0 5.7 fusion.29
  135.0 127.7 %while.54 = (s32[]{:T(128)}, bf16[4,2048,64]{1,2,0:T(8,128)(2,1)}, f32[4,2048]{1,0:T(4,128)S(1)}, bf16[4,2048,64]{2,1,0:T(8,128)(2,1)}, bf16[4,2048,64]{2,1,0:T(...) while((s32[]{:T(128)}, bf16[4,2048,64]{1,2,0:T(8,128)(2,1)}, ...), condition=%wide.region_6.7_spmd, body=%wide.region_1.6_spmd.sunk | while | flops 278990336 | bytes 16777708 | solution.py:155
  138.6 27.0 %while.57 = (s32[]{:T(128)}, bf16[4,512,64]{1,2,0:T(8,128)(2,1)S(1)}, f32[4,512]{1,0:T(4,128)S(1)}, s32[4]{0:T(128)S(1)}, s32[]{:T(128)}, /*index=5*/bf16[2048,6...) while((s32[]{:T(128)}, ...), condition=%wide.region_5.5_spmd, body=%wide.region_2.4_spmd.sunk | while | flops 278990336 | bytes 13598931 | solution.py:83
  141.2 2.3 fusion.119
  147.9 2.3 fusion.119
  154.6 2.3 fusion.119
  161.4 2.3 fusion.119
  170.5 27.0 %while.57 = (s32[]{:T(128)}, bf16[4,512,64]{1,2,0:T(8,128)(2,1)S(1)}, f32[4,512]{1,0:T(4,128)S(1)}, s32[4]{0:T(128)S(1)}, s32[]{:T(128)}, /*index=5*/bf16[2048,6...) while((s32[]{:T(128)}, ...), condition=%wide.region_5.5_spmd, body=%wide.region_2.4_spmd.sunk | while | flops 278990336 | bytes 13598931 | solution.py:83
  173.1 2.3 fusion.119
  179.8 2.3 fusion.119
  186.6 2.3 fusion.119
  193.3 2.3 fusion.119
  202.4 27.0 %while.57 = (s32[]{:T(128)}, bf16[4,512,64]{1,2,0:T(8,128)(2,1)S(1)}, f32[4,512]{1,0:T(4,128)S(1)}, s32[4]{0:T(128)S(1)}, s32[]{:T(128)}, /*index=5*/bf16[2048,6...) while((s32[]{:T(128)}, ...), condition=%wide.region_5.5_spmd, body=%wide.region_2.4_spmd.sunk | while | flops 278990336 | bytes 13598931 | solution.py:83
  205.0 2.3 fusion.119
  211.7 2.3 fusion.119
  218.5 2.3 fusion.119
  225.2 2.3 fusion.119
  234.3 27.0 %while.57 = (s32[]{:T(128)}, bf16[4,512,64]{1,2,0:T(8,128)(2,1)S(1)}, f32[4,512]{1,0:T(4,128)S(1)}, s32[4]{0:T(128)S(1)}, s32[]{:T(128)}, /*index=5*/bf16[2048,6...) while((s32[]{:T(128)}, ...), condition=%wide.region_5.5_spmd, body=%wide.region_2.4_spmd.sunk | while | flops 278990336 | bytes 13598931 | solution.py:83
  236.9 2.3 fusion.119
  243.7 2.3 fusion.119
  250.4 2.3 fusion.119
  257.2 2.3 fusion.119
  262.7 6.7 fusion.66
  271.4 141.2 %reduce-scatter.12.cloned.1.call-done = f32[512,1024]{1,0:T(8,128)} async-done(((f32[2048,1024]{1,0:T(8,128)}), f32[512,1024]{1,0:T(8,128)}) %reduce-scatter.12.cloned.1.call-update) | async-done | bytes 2097168 | tf_op jit(solution)/shard_map/reduce_scatter | solution.py:160
  412.6 1.9 multiply_reduce_fusion.3
  417.9 29.4 %all-gather.14.cloned.1.call-done = bf16[2,1024,704]{1,2,0:T(8,128)(2,1)} async-done(((bf16[2,128,704]{1,2,0:T(8,128)(2,1)}), bf16[2,1024,704]{1,2,0:T(8,128)(2,1)}) %all-gather.14.cloned.1.call-update) | async-done | bytes 2883600 | tf_op jit(solution)/shard_map/all_gather | solution.py:137
  447.3 82.8 %all-gather.12.cloned.1.call-done = bf16[2048,1024]{1,0:T(8,128)(2,1)} async-done(((bf16[512,1024]{1,0:T(8,128)(2,1)}), bf16[2048,1024]{1,0:T(8,128)(2,1)}) %all-gather.12.cloned.1.call-update) | async-done | bytes 4194320 | tf_op jit(solution)/shard_map/all_gather | solution.py:168
  530.1 11.5 convolution_bitcast_fusion.1
  541.6 14.7 all-gather.16.cloned.1.call-done
  556.2 82.4 %all-gather.18.cloned.1.call-done = bf16[2048,1024]{1,0:T(8,128)(2,1)} async-done(((bf16[512,1024]{1,0:T(8,128)(2,1)}), bf16[2048,1024]{1,0:T(8,128)(2,1)}) %all-gather.18.cloned.1.call-update) | async-done | bytes 4194320 | tf_op jit(solution)/shard_map/all_gather | solution.py:191
  638.6 11.3 fusion.37
  652.5 9.0 convolution_bitcast_fusion.2
  661.5 143.1 %reduce-scatter.16.cloned.1.call-done = f32[512,1024]{1,0:T(8,128)} async-done(((f32[2048,1024]{1,0:T(8,128)}), f32[512,1024]{1,0:T(8,128)}) %reduce-scatter.16.cloned.1.call-update) | async-done | bytes 2097168 | tf_op jit(solution)/shard_map/reduce_scatter | solution.py:199
  804.6 2.9 multiply_reduce_fusion.1
  809.5 81.4 %all-gather.20.cloned.1.call-done = bf16[2048,1024]{1,0:T(8,128)(2,1)} async-done(((bf16[512,1024]{1,0:T(8,128)(2,1)}), bf16[2048,1024]{1,0:T(8,128)(2,1)}) %all-gather.20.cloned.1.call-update) | async-done | bytes 4194320 | tf_op jit(solution)/shard_map/all_gather | solution.py:210
  890.9 3.6 fusion.38
  896.3 154.4 %while.56 = (s32[]{:T(128)}, f32[4,2048,64]{1,2,0:T(8,128)}, f32[4,2048,64]{1,2,0:T(8,128)}, f32[4,2048,64]{1,2,0:T(8,128)}, bf16[4,2048,64]{2,1,0:T(8,128)(2,1)...) while((s32[]{:T(128)}, f32[4,2048,64]{1,2,0:T(8,128)}, ...), condition=%wide.region_16.17_spmd, body=%wide.region_12.16_spmd.sunk | while | flops 684197888 | bytes 42895948 | solution.py:216
  901.3 30.0 %while.58 = (s32[]{:T(128)}, f32[2048,64]{0,1:T(8,128)S(1)}, f32[2048,64]{0,1:T(8,128)S(1)}, f32[4,512,64]{1,2,0:T(8,128)}, s32[4]{0:T(128)S(1)}, /*index=5*/s32...) while((s32[]{:T(128)}, f32[2048,64]{0,1:T(8,128)S(1)}, ...), condition=%wide.region_15.15_spmd.clone, body=%wide.region_13.14_spmd.clone.sunk | while | flops 684197888 | bytes 35539192 | solution.py:113
  939.9 30.0 %while.58 = (s32[]{:T(128)}, f32[2048,64]{0,1:T(8,128)S(1)}, f32[2048,64]{0,1:T(8,128)S(1)}, f32[4,512,64]{1,2,0:T(8,128)}, s32[4]{0:T(128)S(1)}, /*index=5*/s32...) while((s32[]{:T(128)}, f32[2048,64]{0,1:T(8,128)S(1)}, ...), condition=%wide.region_15.15_spmd.clone, body=%wide.region_13.14_spmd.clone.sunk | while | flops 684197888 | bytes 35539192 | solution.py:113
  978.5 30.0 %while.58 = (s32[]{:T(128)}, f32[2048,64]{0,1:T(8,128)S(1)}, f32[2048,64]{0,1:T(8,128)S(1)}, f32[4,512,64]{1,2,0:T(8,128)}, s32[4]{0:T(128)S(1)}, /*index=5*/s32...) while((s32[]{:T(128)}, f32[2048,64]{0,1:T(8,128)S(1)}, ...), condition=%wide.region_15.15_spmd.clone, body=%wide.region_13.14_spmd.clone.sunk | while | flops 684197888 | bytes 35539192 | solution.py:113
  1017.1 30.0 %while.58 = (s32[]{:T(128)}, f32[2048,64]{0,1:T(8,128)S(1)}, f32[2048,64]{0,1:T(8,128)S(1)}, f32[4,512,64]{1,2,0:T(8,128)}, s32[4]{0:T(128)S(1)}, /*index=5*/s32...) while((s32[]{:T(128)}, f32[2048,64]{0,1:T(8,128)S(1)}, ...), condition=%wide.region_15.15_spmd.clone, body=%wide.region_13.14_spmd.clone.sunk | while | flops 684197888 | bytes 35539192 | solution.py:113
  1050.7 3.9 subtract_convert_fusion.1
  1062.3 7.1 bitcast_convert_fusion
  1070.7 7.4 fusion.52
  1079.5 6.9 convolution_convert_fusion
  1086.5 58.5 %reduce-scatter.18.cloned.1.call-done = bf16[512,1024]{1,0:T(8,128)(2,1)} async-done(((bf16[2048,1024]{1,0:T(8,128)(2,1)}), bf16[512,1024]{1,0:T(8,128)(2,1)}) %reduce-scatter.18.cloned.1.call-update) | async-done | bytes 1048592 | tf_op jit(solution)/shard_map/reduce_scatter | solution.py:228
  1144.9 2.0 fusion.47
  1148.1 7.8 fusion.68
  1156.0 11.5 fusion.39
  1168.7 4.4 fusion.67
  1173.2 3.0 copy.77
  1176.2 19.3 %reduce-scatter.20.cloned.1.call-done = f32[3,128,256]{1,2,0:T(8,128)} async-done(((f32[3,1024,256]{1,2,0:T(8,128)}), f32[3,128,256]{1,2,0:T(8,128)}) %reduce-scatter.20.cloned.1.call-update) | async-done | bytes 393232 | tf_op jit(solution)/shard_map/reduce_scatter | solution.py:242
  1195.5 1.9 copy.78
  1197.4 77.0 %reduce-scatter.14.cloned.1.call-done = bf16[512,1024]{1,0:T(8,128)(2,1)} async-done(((bf16[2048,1024]{1,0:T(8,128)(2,1)}), bf16[512,1024]{1,0:T(8,128)(2,1)}) %reduce-scatter.14.cloned.1.call-update) | async-done | bytes 1048592 | tf_op jit(solution)/shard_map/reduce_scatter | solution.py:176
  1274.5 4.3 fusion.44
  1278.7 33.8 %reduce-scatter.28.cloned.1.call-done = f32[128,2]{1,0:T(8,128)} async-done(((f32[1024,2]{1,0:T(8,128)}), f32[128,2]{1,0:T(8,128)}) %reduce-scatter.28.cloned.1.call-update) | async-done | bytes 1040
  1313.4 12.2 psum.7
  1325.6 35.6 %reduce-scatter.26.cloned.1.call-done = f32[704,128]{1,0:T(8,128)} async-done(((f32[704,1024]{1,0:T(8,128)}), f32[704,128]{1,0:T(8,128)}) %reduce-scatter.26.cloned.1.call-update) | async-done | bytes 360464 | tf_op jit(solution)/shard_map/reduce_scatter | solution.py:245
  1361.2 63.3 %reduce-scatter.24.cloned.1.call-done = f32[2,128,704]{1,2,0:T(8,128)} async-done(((f32[2,1024,704]{1,2,0:T(8,128)}), f32[2,128,704]{1,2,0:T(8,128)}) %reduce-scatter.24.cloned.1.call-update) | async-done | bytes 720912 | tf_op jit(solution)/shard_map/reduce_scatter | solution.py:244
  1424.5 39.6 %reduce-scatter.22.cloned.1.call-done = f32[256,128]{1,0:T(8,128)} async-done(((f32[256,1024]{1,0:T(8,128)}), f32[256,128]{1,0:T(8,128)}) %reduce-scatter.22.cloned.1.call-update) | async-done | bytes 131088 | tf_op jit(solution)/shard_map/reduce_scatter | solution.py:243
  (529 shorter events, 262.1 us)
Async XLA Ops:
  7.2 15.1 %copy-start.2 = (bf16[512,1024]{1,0:T(8,128)(2,1)S(1)}, bf16[512,1024]{1,0:T(8,128)(2,1)}, u32[]{:S(2)}) copy-start(bf16[512,1024]{1,0:T(8,128)(2,1)} %param.17) | copy-start | bytes 3145732
  7.2 32.6 %all-gather.10.cloned.1.call-start = ((), (), s32[]{:S(2)}) async-start(), calls=%async_computation.10 | async-start | bytes 1769472 | tf_op jit(solution)/shard_map/all_gather | solution.py:135
  9.1 113.8 %all-gather.8.cloned.1.call-start = ((), (), s32[]{:S(2)}) async-start(), calls=%async_computation.9 | async-start | bytes 5242880 | tf_op jit(solution)/shard_map/all_gather | solution.py:146
  20.1 4.3 copy-start.18
  20.1 4.3 copy-start.12
  21.7 2.6 copy-start.25
  22.3 2.0 copy-start.21
  23.6 389.0 %reduce-scatter.12.cloned.1.call-start = ((), (), s32[]{:S(2)}) async-start(), calls=%async_computation.11 | async-start | bytes 10485760 | tf_op jit(solution)/shard_map/reduce_scatter | solution.py:160
  38.8 90.7 %copy-start.8 = (f32[2048,32]{0,1:T(8,128)}, f32[2048,32]{0,1:T(8,128)S(1)}, u32[]{:S(2)}) copy-start(f32[2048,32]{0,1:T(8,128)S(1)} %get-tuple-element.429) | copy-start | bytes 786436
  262.7 6.7 copy-start.5
  269.4 1.1 copy-start.16
  269.4 143.2 %copy-start.3 = (bf16[512,1024]{1,0:T(8,128)(2,1)S(1)}, bf16[512,1024]{1,0:T(8,128)(2,1)}, u32[]{:S(2)}) copy-start(bf16[512,1024]{1,0:T(8,128)(2,1)} %param.17) | copy-start | bytes 3145732
  269.4 177.9 %all-gather.14.cloned.1.call-start = ((), (), s32[]{:S(2)}) async-start(), calls=%async_computation.13 | async-start | bytes 3244032 | tf_op jit(solution)/shard_map/all_gather | solution.py:137
  271.3 143.2 %copy-start.19 = (f32[1,1024]{1,0:T(1,128)S(1)}, f32[1,1024]{1,0:T(1,128)}, u32[]{:S(2)}) copy-start(f32[1,1024]{1,0:T(1,128)} %get-tuple-element.425) | copy-start | bytes 12292
  271.3 258.8 %all-gather.12.cloned.1.call-start = ((), (), s32[]{:S(2)}) async-start(), calls=%async_computation.12 | async-start | bytes 5242880 | tf_op jit(solution)/shard_map/all_gather | solution.py:168
  414.5 393.0 %copy-start = (f32[512,1024]{1,0:T(8,128)}, f32[512,1024]{1,0:T(8,128)S(1)}, u32[]{:S(2)}) copy-start(f32[512,1024]{1,0:T(8,128)S(1)} %get-tuple-element.395) | copy-start | bytes 6291460
  414.5 393.0 %copy-start.23 = (f32[512]{0:T(512)}, f32[512]{0:T(512)S(1)}, u32[]{:S(2)}) copy-start(f32[512]{0:T(512)S(1)} %add_rsqrt_fusion) | copy-start | bytes 6148
  414.6 1.3 copy-start.17
  415.8 140.4 %all-gather.16.cloned.1.call-start = ((), (), s32[]{:S(2)}) async-start(), calls=%async_computation.14 | async-start | bytes 1622016 | tf_op jit(solution)/shard_map/all_gather | solution.py:138
  416.6 222.0 %all-gather.18.cloned.1.call-start = ((), (), s32[]{:S(2)}) async-start(), calls=%async_computation.16 | async-start | bytes 5242880 | tf_op jit(solution)/shard_map/all_gather | solution.py:191
  417.3 387.3 %reduce-scatter.16.cloned.1.call-start = ((), (), s32[]{:S(2)}) async-start(), calls=%async_computation.17 | async-start | bytes 10485760 | tf_op jit(solution)/shard_map/reduce_scatter | solution.py:199
  638.6 13.9 copy-start.30
  649.9 1.5 copy-start.32
  649.9 2.5 copy-start.33
  661.5 146.1 %copy-start.7 = (bf16[512,1024]{1,0:T(8,128)(2,1)S(1)}, bf16[512,1024]{1,0:T(8,128)(2,1)}, u32[]{:S(2)}) copy-start(bf16[512,1024]{1,0:T(8,128)(2,1)} %param.25) | copy-start | bytes 3145732
  661.5 229.4 %all-gather.20.cloned.1.call-start = ((), (), s32[]{:S(2)}) async-start(), calls=%async_computation.18 | async-start | bytes 5242880 | tf_op jit(solution)/shard_map/all_gather | solution.py:210
  804.6 2.9 copy-start.6
  807.6 1.6 copy-start.27
  809.2 335.7 %reduce-scatter.18.cloned.1.call-start = ((), (), s32[]{:S(2)}) async-start(), calls=%async_computation.19 | async-start | bytes 5242880 | tf_op jit(solution)/shard_map/reduce_scatter | solution.py:228
  896.3 154.5 %copy-start.9 = (f32[2048,32]{0,1:T(8,128)S(1)}, f32[2048,32]{0,1:T(8,128)}, u32[]{:S(2)}) copy-start(f32[2048,32]{0,1:T(8,128)} %copy-done.8) | copy-start | bytes 786436
  1056.0 2.8 copy-start.10
  1060.4 1.3 copy-start.13
  1060.4 1.9 copy-start.14
  1069.5 1.2 copy-start.15
  1069.5 126.0 %reduce-scatter.20.cloned.1.call-start = ((), (), s32[]{:S(2)}) async-start(), calls=%async_computation.20 | async-start | bytes 3538944 | tf_op jit(solution)/shard_map/reduce_scatter | solution.py:242
  1078.1 1.4 copy-start.31
  1078.2 196.3 %reduce-scatter.14.cloned.1.call-start = ((), (), s32[]{:S(2)}) async-start(), calls=%async_computation.15 | async-start | bytes 5242880 | tf_op jit(solution)/shard_map/reduce_scatter | solution.py:176
  1086.4 58.5 %copy-start.4 = (bf16[512,1024]{1,0:T(8,128)(2,1)S(1)}, bf16[512,1024]{1,0:T(8,128)(2,1)}, u32[]{:S(2)}) copy-start(bf16[512,1024]{1,0:T(8,128)(2,1)} %param.17) | copy-start | bytes 3145732
  1086.4 58.5 %copy-start.22 = (f32[1,1024]{1,0:T(1,128)S(1)}, f32[1,1024]{1,0:T(1,128)}, u32[]{:S(2)}) copy-start(f32[1,1024]{1,0:T(1,128)} %copy-done.21) | copy-start | bytes 12292
  1086.4 58.5 %copy-start.26 = (f32[512]{0:T(512)S(1)}, f32[512]{0:T(512)}, u32[]{:S(2)}) copy-start(f32[512]{0:T(512)} %copy-done.25) | copy-start | bytes 6148
  1086.4 60.6 %copy-start.29 = (f32[1024]{0:T(1024)S(1)}, f32[1024]{0:T(1024)}, u32[]{:S(2)}) copy-start(f32[1024]{0:T(1024)} %get-tuple-element.318) | copy-start | bytes 12292
  1086.4 226.1 %reduce-scatter.28.cloned.1.call-start = ((), (), s32[]{:S(2)}) async-start(), calls=%async_computation.24 | async-start | bytes 589824
  1148.1 213.1 %reduce-scatter.26.cloned.1.call-start = ((), (), s32[]{:S(2)}) async-start(), calls=%async_computation.23 | async-start | bytes 3244032 | tf_op jit(solution)/shard_map/reduce_scatter | solution.py:245
  1155.9 268.6 %reduce-scatter.24.cloned.1.call-start = ((), (), s32[]{:S(2)}) async-start(), calls=%async_computation.22 | async-start | bytes 6488064 | tf_op jit(solution)/shard_map/reduce_scatter | solution.py:244
  1167.5 1.2 copy-start.11
  1167.5 296.6 %reduce-scatter.22.cloned.1.call-start = ((), (), s32[]{:S(2)}) async-start(), calls=%async_computation.21 | async-start | bytes 1179648 | tf_op jit(solution)/shard_map/reduce_scatter | solution.py:243
  1173.2 101.3 %copy-start.1 = (f32[512,1024]{1,0:T(8,128)S(1)}, f32[512,1024]{1,0:T(8,128)}, u32[]{:S(2)}) copy-start(f32[512,1024]{1,0:T(8,128)} %copy-done) | copy-start | bytes 6291460
  1173.2 101.3 %copy-start.20 = (f32[1,1024]{1,0:T(1,128)S(1)}, f32[1,1024]{1,0:T(1,128)}, u32[]{:S(2)}) copy-start(f32[1,1024]{1,0:T(1,128)} %get-tuple-element.425) | copy-start | bytes 12292
  1173.2 101.3 %copy-start.24 = (f32[512]{0:T(512)S(1)}, f32[512]{0:T(512)}, u32[]{:S(2)}) copy-start(f32[512]{0:T(512)} %copy-done.23) | copy-start | bytes 6148
  1173.2 101.2 %copy-start.28 = (f32[512]{0:T(512)S(1)}, f32[512]{0:T(512)}, u32[]{:S(2)}) copy-start(f32[512]{0:T(512)} %copy-done.27) | copy-start | bytes 6148
Sparse Core Ops, SparseCore 0:
  10.5 29.2 all-gather.9
  41.9 80.9 all-gather.7
  269.5 143.0 reduce-scatter.11
  414.9 32.3 all-gather.13
  449.3 80.7 all-gather.11
  532.4 23.8 all-gather.15
  557.8 80.7 all-gather.17
  661.6 143.0 reduce-scatter.15
  809.4 81.4 all-gather.19
  1069.6 75.2 reduce-scatter.17
  1148.7 46.7 reduce-scatter.19
  1197.7 76.7 reduce-scatter.13
  1277.8 34.6 reduce-scatter.27
  1316.3 44.8 reduce-scatter.25
  1365.5 58.9 reduce-scatter.23
  1428.1 35.9 reduce-scatter.21
where the time goes:
time: 1480 us; the launch traced here: 1470 us
  waiting for transfers between devices  987 us (67%)
  matrix products  226 us (15%)
  local copies, waits for them, and re-layouts  102 us (7%)
  other arithmetic  81.1 us (5%)
  blocking collectives  34.4 us (2%)
  loops' own time  22.6 us (2%)
  between operations  15.4 us (1%)
    reduce_scatter x1, waiting for transfers between devices, shards(): lax.psum_scatter(jnp.einsum('ktf,kdf->td', piece, gates_back, preferred_e...  143 us
    reduce_scatter x1, waiting for transfers between devices, shards(): lax.psum_scatter(jnp.dot(piece, proj_full, preferred_element_type=jnp.flo...  141 us
    all_gather x1, waiting for transfers between devices, shards(): lax.all_gather(normed_a.astype(jnp.bfloat16), 'head', axis=0, tiled=True)  83.2 us
    all_gather x1, waiting for transfers between devices, shards(): lax.all_gather(normed_b.astype(jnp.bfloat16), 'head', axis=0, tiled=True)  82.8 us
    all_gather x1, waiting for transfers between devices, shards(): piece = lax.all_gather(cotangent, 'head', axis=0, tiled=True)  82.4 us
    all_gather x1, waiting for transfers between devices, shards(): piece = lax.all_gather(branch_grad, 'head', axis=0, tiled=True)  81.4 us
    reduce_scatter x1, waiting for transfers between devices, shards(): lax.psum_scatter(jnp.dot(piece, down_full, preferred_element_type=jnp.flo...  77 us
    reduce_scatter x1, waiting for transfers between devices, shards(): lax.psum_scatter(gates_part, 'dp', scatter_dimension=1, tiled=True)  63.3 us
  transfers between devices with their start and end apart: 16, of which 16 were waited for; matrix products, arithmetic and copies ran while one was open for 5% of the time, Pallas kernels for 0%

commit v1 on v0

--- a/solution.py
+++ b/solution.py
@@ -188,7 +188,39 @@
         lax.all_gather(gain_low, "dp", axis=1, tiled=True),
     )
     qkv_back, proj_back, gates_back, down_back, gain_back = back_full
-    piece = lax.all_gather(cotangent, "head", axis=0, tiled=True)
+    arr_next, s_next, right_arr = (
+        jax.lax.axis_size("head"),
+        jax.lax.axis_index("head"),
+        cotangent.shape[0],
+    )
+    history = []
+    dev = 0
+    while dev < arr_next:
+        history.append((dev, (dev + 1) % arr_next))
+        dev = dev + 1
+    seen = []
+    dev = 0
+    while dev < arr_next:
+        seen.append((dev, (dev - 1) % arr_next))
+        dev += 1
+    piece = jnp.zeros(
+        (*cotangent.shape[:0], arr_next * right_arr, *cotangent.shape[0 + 1 :]), cotangent.dtype
+    )
+    piece = lax.dynamic_update_slice_in_dim(piece, cotangent, s_next * right_arr, axis=0)
+    prior = reply = cotangent
+    next_value = arr_next // 2
+    hop_no = 1
+    while hop_no < next_value + 1:
+        prior = jax.lax.ppermute(prior, "head", history)
+        piece = lax.dynamic_update_slice_in_dim(
+            piece, prior, (s_next - hop_no) % arr_next * right_arr, axis=0
+        )
+        if hop_no < arr_next - next_value:
+            reply = jax.lax.ppermute(reply, axis_name="head", perm=seen)
+            piece = lax.dynamic_update_slice_in_dim(
+                piece, reply, (s_next + hop_no) % arr_next * right_arr, axis=0
+            )
+        hop_no = hop_no + 1
     down_sum = jnp.einsum("tf,td->fd", inner, piece, preferred_element_type=jnp.float32)
     rows_grad = jnp.einsum("td,fd->tf", piece, down_back, preferred_element_type=jnp.float32)
     inner_grad = rows_grad

time: 1480 us -> 1430 us (0.966)
  waiting for transfers between devices: 987 us -> 891 us
  starting transfers between devices: 1.82 us -> 31.1 us
    all_gather x1 -> x0, waiting for transfers between devices: 82.4 us -> none  [shards(): piece = lax.all_gather(cotangent, 'head', axis=0, tiled=True)]
    ppermute x0 -> x3, waiting for transfers between devices: none -> 60.1 us  [the longest x2 56.8 us: shards(): prior = jax.lax.ppermute(prior, 'head', history)]
    all_gather x1, waiting for transfers between devices: 82.8 us -> 38.5 us  [shards(): lax.all_gather(normed_b.astype(jnp.bfloat16), 'head', axis=0, tiled=True)]
    ppermute x0 -> x3, starting transfers between devices: none -> 29.8 us  [the longest x2 26.6 us: shards(): prior = jax.lax.ppermute(prior, 'head', history)]
    all_gather x1, waiting for transfers between devices: 29.4 us -> 0.01 us  [shards(): lax.all_gather(gates_low, 'dp', axis=1, tiled=True)]
    unnamed x17 -> x16, waiting for transfers between devices: 34.7 us -> 33.9 us
  transfers between devices with their start and end apart: 16 -> 18, of which waited for: 16 -> 16; matrix products, arithmetic and copies ran while one was open for 5% -> 6% of each run, Pallas kernels for 0% -> 0%
where the time goes in v1:
time: 1430 us; the launch traced here: 1420 us
  waiting for transfers between devices  891 us (62%)
  matrix products  227 us (16%)
  local copies, waits for them, and re-layouts  113 us (8%)
  other arithmetic  82.6 us (6%)
  blocking collectives  35.4 us (2%)
  starting transfers between devices  31.1 us (2%)
  loops' own time  22.5 us (2%)
  between operations  15.4 us (1%)
    reduce_scatter x1, waiting for transfers between devices, shards(): lax.psum_scatter(jnp.einsum('ktf,kdf->td', piece, gates_back, preferred_e...  145 us
    reduce_scatter x1, waiting for transfers between devices, shards(): lax.psum_scatter(jnp.dot(piece, proj_full, preferred_element_type=jnp.flo...  141 us
    all_gather x1, waiting for transfers between devices, shards(): lax.all_gather(normed_a.astype(jnp.bfloat16), 'head', axis=0, tiled=True)  81.9 us
    all_gather x1, waiting for transfers between devices, shards(): piece = lax.all_gather(branch_grad, 'head', axis=0, tiled=True)  81.4 us
    reduce_scatter x1, waiting for transfers between devices, shards(): lax.psum_scatter(jnp.dot(piece, down_full, preferred_element_type=jnp.flo...  77.2 us
    reduce_scatter x1, waiting for transfers between devices, shards(): lax.psum_scatter(gates_part, 'dp', scatter_dimension=1, tiled=True)  63.3 us
    dot_general x32, matrix products, block_scores(): jnp.einsum('qe,ke->qk', query_block, keys, preferred_element_type=jnp.flo...  61.9 us
    reduce_scatter x1, waiting for transfers between devices, shards(): lax.psum_scatter(jnp.einsum('ktc,kdc->td', piece, qkv_back, preferred_ele...  58.1 us
  transfers between devices with their start and end apart: 18, of which 16 were waited for; matrix products, arithmetic and copies ran while one was open for 6% of the time, Pallas kernels for 0%

profile of v1, /device:TPU:0, one launch (start us, length us, event | category | flops | bytes accessed | tf_op | source)
XLA Modules:
  0.0 1417.8 jit_solution(1695647114268749028)
XLA Ops:
  9.9 10.2 all_gather.29
  22.8 2.5 fusion.45
  26.7 13.0 all_gather.32
  41.6 81.9 %all-gather.7.cloned.1.call-done = bf16[2048,1024]{1,0:T(8,128)(2,1)} async-done(((bf16[512,1024]{1,0:T(8,128)(2,1)}), bf16[2048,1024]{1,0:T(8,128)(2,1)}) %all-gather.7.cloned.1.call-update) | async-done | bytes 4194320 | tf_op jit(solution)/shard_map/all_gather | solution.py:146
  123.4 5.7 fusion.29
  135.4 127.7 %while.54 = (s32[]{:T(128)}, bf16[4,2048,64]{1,2,0:T(8,128)(2,1)}, f32[4,2048]{1,0:T(4,128)S(1)}, bf16[4,2048,64]{2,1,0:T(8,128)(2,1)}, bf16[4,2048,64]{2,1,0:T(...) while((s32[]{:T(128)}, bf16[4,2048,64]{1,2,0:T(8,128)(2,1)}, ...), condition=%wide.region_6.7_spmd, body=%wide.region_1.6_spmd.sunk | while | flops 278990336 | bytes 16777708 | solution.py:155
  139.0 27.0 %while.57 = (s32[]{:T(128)}, bf16[4,512,64]{1,2,0:T(8,128)(2,1)S(1)}, f32[4,512]{1,0:T(4,128)S(1)}, s32[4]{0:T(128)S(1)}, s32[]{:T(128)}, /*index=5*/bf16[2048,6...) while((s32[]{:T(128)}, ...), condition=%wide.region_5.5_spmd, body=%wide.region_2.4_spmd.sunk | while | flops 278990336 | bytes 13598931 | solution.py:83
  141.6 2.3 fusion.119
  148.3 2.3 fusion.119
  155.1 2.3 fusion.119
  161.8 2.3 fusion.119
  170.9 27.0 %while.57 = (s32[]{:T(128)}, bf16[4,512,64]{1,2,0:T(8,128)(2,1)S(1)}, f32[4,512]{1,0:T(4,128)S(1)}, s32[4]{0:T(128)S(1)}, s32[]{:T(128)}, /*index=5*/bf16[2048,6...) while((s32[]{:T(128)}, ...), condition=%wide.region_5.5_spmd, body=%wide.region_2.4_spmd.sunk | while | flops 278990336 | bytes 13598931 | solution.py:83
  173.5 2.3 fusion.119
  180.3 2.3 fusion.119
  187.0 2.3 fusion.119
  193.7 2.3 fusion.119
  202.8 27.0 %while.57 = (s32[]{:T(128)}, bf16[4,512,64]{1,2,0:T(8,128)(2,1)S(1)}, f32[4,512]{1,0:T(4,128)S(1)}, s32[4]{0:T(128)S(1)}, s32[]{:T(128)}, /*index=5*/bf16[2048,6...) while((s32[]{:T(128)}, ...), condition=%wide.region_5.5_spmd, body=%wide.region_2.4_spmd.sunk | while | flops 278990336 | bytes 13598931 | solution.py:83
  205.4 2.3 fusion.119
  212.2 2.3 fusion.119
  218.9 2.3 fusion.119
  225.7 2.3 fusion.119
  234.8 27.0 %while.57 = (s32[]{:T(128)}, bf16[4,512,64]{1,2,0:T(8,128)(2,1)S(1)}, f32[4,512]{1,0:T(4,128)S(1)}, s32[4]{0:T(128)S(1)}, s32[]{:T(128)}, /*index=5*/bf16[2048,6...) while((s32[]{:T(128)}, ...), condition=%wide.region_5.5_spmd, body=%wide.region_2.4_spmd.sunk | while | flops 278990336 | bytes 13598931 | solution.py:83
  237.4 2.3 fusion.119
  244.1 2.3 fusion.119
  250.8 2.3 fusion.119
  263.1 6.7 fusion.66
  271.8 141.2 %reduce-scatter.12.cloned.1.call-done = f32[512,1024]{1,0:T(8,128)} async-done(((f32[2048,1024]{1,0:T(8,128)}), f32[512,1024]{1,0:T(8,128)}) %reduce-scatter.12.cloned.1.call-update) | async-done | bytes 2097168 | tf_op jit(solution)/shard_map/reduce_scatter | solution.py:160
  418.1 3.2 collective-permute-start.1
  422.1 22.9 %collective-permute-done = bf16[512,1024]{1,0:T(8,128)(2,1)} collective-permute-done((bf16[512,1024]{1,0:T(8,128)(2,1)S(1)}, bf16[512,1024]{1,0:T(8,128)(2,1)}, u32[]{:S(2)}, u32[]{:S(2)}) %collective-permute-start) | collective-permute-done | bytes 1048608 | tf_op jit(solution)/shard_map/ppermute | solution.py:214
  445.0 25.5 %collective-permute-start.2 = (bf16[512,1024]{1,0:T(8,128)(2,1)}, bf16[512,1024]{1,0:T(8,128)(2,1)}, u32[]{:S(2)}, u32[]{:S(2)}) collective-permute-start(bf16[512,1024]{1,0:T(8,128)(2,1)} %collective-permute-done), channel_id=1, source_target_pairs={{0,1},{1,2},{2,3},{3,0},{4,5},{5,6},{6,7},{7,4},{8,9},{9,10},{10,1... | collective-permute-start | bytes 3145736 | tf_op jit(solution)/shard_map/ppermute | solution.py:214
  470.4 2.5 broadcast_in_dim.70
  476.2 3.3 collective-permute-done.1
  481.8 33.9 %collective-permute-done.2 = bf16[512,1024]{1,0:T(8,128)(2,1)} collective-permute-done((bf16[512,1024]{1,0:T(8,128)(2,1)}, bf16[512,1024]{1,0:T(8,128)(2,1)}, u32[]{:S(2)}, u32[]{:S(2)}) %collective-permute-start.2) | collective-permute-done | bytes 1048608 | tf_op jit(solution)/shard_map/ppermute | solution.py:214
  518.0 38.5 %all-gather.11.cloned.1.call-done = bf16[2048,1024]{1,0:T(8,128)(2,1)} async-done(((bf16[512,1024]{1,0:T(8,128)(2,1)}), bf16[2048,1024]{1,0:T(8,128)(2,1)}) %all-gather.11.cloned.1.call-update) | async-done | bytes 4194320 | tf_op jit(solution)/shard_map/all_gather | solution.py:168
  556.5 11.5 convolution_bitcast_fusion.1
  567.9 16.0 %all-gather.15.cloned.1.call-done = bf16[704,1024]{1,0:T(8,128)(2,1)} async-done(((bf16[704,128]{1,0:T(8,128)(2,1)}), bf16[704,1024]{1,0:T(8,128)(2,1)}) %all-gather.15.cloned.1.call-update) | async-done | bytes 1441808 | tf_op jit(solution)/shard_map/all_gather | solution.py:138
  583.9 11.3 fusion.37
  597.8 9.0 convolution_bitcast_fusion.2
  606.9 144.6 %reduce-scatter.16.cloned.1.call-done = f32[512,1024]{1,0:T(8,128)} async-done(((f32[2048,1024]{1,0:T(8,128)}), f32[512,1024]{1,0:T(8,128)}) %reduce-scatter.16.cloned.1.call-update) | async-done | bytes 2097168 | tf_op jit(solution)/shard_map/reduce_scatter | solution.py:231
  751.5 2.9 multiply_reduce_fusion.1
  756.3 81.4 %all-gather.17.cloned.1.call-done = bf16[2048,1024]{1,0:T(8,128)(2,1)} async-done(((bf16[512,1024]{1,0:T(8,128)(2,1)}), bf16[2048,1024]{1,0:T(8,128)(2,1)}) %all-gather.17.cloned.1.call-update) | async-done | bytes 4194320 | tf_op jit(solution)/shard_map/all_gather | solution.py:242
  837.7 3.6 fusion.38
  843.1 155.5 %while.56 = (s32[]{:T(128)}, f32[4,2048,64]{1,2,0:T(8,128)}, f32[4,2048,64]{1,2,0:T(8,128)}, f32[4,2048,64]{1,2,0:T(8,128)}, bf16[4,2048,64]{2,1,0:T(8,128)(2,1)...) while((s32[]{:T(128)}, f32[4,2048,64]{1,2,0:T(8,128)}, ...), condition=%wide.region_16.17_spmd, body=%wide.region_12.16_spmd.sunk | while | flops 684197888 | bytes 42895948 | solution.py:248
  848.1 30.3 %while.58 = (s32[]{:T(128)}, f32[2048,64]{0,1:T(8,128)S(1)}, f32[2048,64]{0,1:T(8,128)S(1)}, f32[4,512,64]{1,2,0:T(8,128)}, s32[4]{0:T(128)S(1)}, /*index=5*/s32...) while((s32[]{:T(128)}, f32[2048,64]{0,1:T(8,128)S(1)}, ...), condition=%wide.region_15.15_spmd.clone, body=%wide.region_13.14_spmd.clone.sunk | while | flops 684197888 | bytes 35539192 | solution.py:113
  887.0 30.3 %while.58 = (s32[]{:T(128)}, f32[2048,64]{0,1:T(8,128)S(1)}, f32[2048,64]{0,1:T(8,128)S(1)}, f32[4,512,64]{1,2,0:T(8,128)}, s32[4]{0:T(128)S(1)}, /*index=5*/s32...) while((s32[]{:T(128)}, f32[2048,64]{0,1:T(8,128)S(1)}, ...), condition=%wide.region_15.15_spmd.clone, body=%wide.region_13.14_spmd.clone.sunk | while | flops 684197888 | bytes 35539192 | solution.py:113
  925.9 30.3 %while.58 = (s32[]{:T(128)}, f32[2048,64]{0,1:T(8,128)S(1)}, f32[2048,64]{0,1:T(8,128)S(1)}, f32[4,512,64]{1,2,0:T(8,128)}, s32[4]{0:T(128)S(1)}, /*index=5*/s32...) while((s32[]{:T(128)}, f32[2048,64]{0,1:T(8,128)S(1)}, ...), condition=%wide.region_15.15_spmd.clone, body=%wide.region_13.14_spmd.clone.sunk | while | flops 684197888 | bytes 35539192 | solution.py:113
  964.8 30.3 %while.58 = (s32[]{:T(128)}, f32[2048,64]{0,1:T(8,128)S(1)}, f32[2048,64]{0,1:T(8,128)S(1)}, f32[4,512,64]{1,2,0:T(8,128)}, s32[4]{0:T(128)S(1)}, /*index=5*/s32...) while((s32[]{:T(128)}, f32[2048,64]{0,1:T(8,128)S(1)}, ...), condition=%wide.region_15.15_spmd.clone, body=%wide.region_13.14_spmd.clone.sunk | while | flops 684197888 | bytes 35539192 | solution.py:113
  998.6 3.8 subtract_convert_fusion.1
  1008.7 7.5 bitcast_convert_fusion
  1017.7 7.4 fusion.52
  1026.5 6.9 convolution_convert_fusion
  1033.5 58.1 %reduce-scatter.18.cloned.1.call-done = bf16[512,1024]{1,0:T(8,128)(2,1)} async-done(((bf16[2048,1024]{1,0:T(8,128)(2,1)}), bf16[512,1024]{1,0:T(8,128)(2,1)}) %reduce-scatter.18.cloned.1.call-update) | async-done | bytes 1048592 | tf_op jit(solution)/shard_map/reduce_scatter | solution.py:260
  1094.8 7.7 fusion.68
  1102.6 11.5 fusion.39
  1115.4 4.5 fusion.67
  1119.9 3.0 copy.77
  1122.9 19.1 %reduce-scatter.20.cloned.1.call-done = f32[3,128,256]{1,2,0:T(8,128)} async-done(((f32[3,1024,256]{1,2,0:T(8,128)}), f32[3,128,256]{1,2,0:T(8,128)}) %reduce-scatter.20.cloned.1.call-update) | async-done | bytes 393232 | tf_op jit(solution)/shard_map/reduce_scatter | solution.py:274
  1143.9 77.2 %reduce-scatter.14.cloned.1.call-done = bf16[512,1024]{1,0:T(8,128)(2,1)} async-done(((bf16[2048,1024]{1,0:T(8,128)(2,1)}), bf16[512,1024]{1,0:T(8,128)(2,1)}) %reduce-scatter.14.cloned.1.call-update) | async-done | bytes 1048592 | tf_op jit(solution)/shard_map/reduce_scatter | solution.py:176
  1221.1 4.3 fusion.44
  1225.4 33.7 %reduce-scatter.28.cloned.1.call-done = f32[128,2]{1,0:T(8,128)} async-done(((f32[1024,2]{1,0:T(8,128)}), f32[128,2]{1,0:T(8,128)}) %reduce-scatter.28.cloned.1.call-update) | async-done | bytes 1040
  1259.9 12.2 psum.7
  1272.2 35.7 %reduce-scatter.26.cloned.1.call-done = f32[704,128]{1,0:T(8,128)} async-done(((f32[704,1024]{1,0:T(8,128)}), f32[704,128]{1,0:T(8,128)}) %reduce-scatter.26.cloned.1.call-update) | async-done | bytes 360464 | tf_op jit(solution)/shard_map/reduce_scatter | solution.py:277
  1307.9 63.3 %reduce-scatter.24.cloned.1.call-done = f32[2,128,704]{1,2,0:T(8,128)} async-done(((f32[2,1024,704]{1,2,0:T(8,128)}), f32[2,128,704]{1,2,0:T(8,128)}) %reduce-scatter.24.cloned.1.call-update) | async-done | bytes 720912 | tf_op jit(solution)/shard_map/reduce_scatter | solution.py:276
  1371.2 39.6 %reduce-scatter.22.cloned.1.call-done = f32[256,128]{1,0:T(8,128)} async-done(((f32[256,1024]{1,0:T(8,128)}), f32[256,128]{1,0:T(8,128)}) %reduce-scatter.22.cloned.1.call-update) | async-done | bytes 131088 | tf_op jit(solution)/shard_map/reduce_scatter | solution.py:275
  (533 shorter events, 278.8 us)
Async XLA Ops:
  7.2 18.9 %copy-start.16 = (f32[256,128]{1,0:T(8,128)S(1)}, f32[256,128]{1,0:T(8,128)}, u32[]{:S(2)}) copy-start(f32[256,128]{1,0:T(8,128)} %param.20) | copy-start | bytes 393220
  7.2 18.9 %copy-start.11 = (bf16[2048,256]{1,0:T(8,128)(2,1)S(1)}, bf16[2048,256]{1,0:T(8,128)(2,1)}, u32[]{:S(2)}) copy-start(bf16[2048,256]{1,0:T(8,128)(2,1)} %param.18) | copy-start | bytes 3145732
  7.2 34.4 %all-gather.9.cloned.1.call-start = ((), (), s32[]{:S(2)}) async-start(), calls=%async_computation.10 | async-start | bytes 1769472 | tf_op jit(solution)/shard_map/all_gather | solution.py:135
  9.2 114.3 %all-gather.7.cloned.1.call-start = ((), (), s32[]{:S(2)}) async-start(), calls=%async_computation.9 | async-start | bytes 5242880 | tf_op jit(solution)/shard_map/all_gather | solution.py:146
  21.6 0.6 copy-start.23
  22.2 0.6 copy-start.19
  25.3 387.7 %reduce-scatter.12.cloned.1.call-start = ((), (), s32[]{:S(2)}) async-start(), calls=%async_computation.11 | async-start | bytes 10485760 | tf_op jit(solution)/shard_map/reduce_scatter | solution.py:160
  41.5 88.4 %copy-start.7 = (f32[2048,32]{0,1:T(8,128)}, f32[2048,32]{0,1:T(8,128)S(1)}, u32[]{:S(2)}) copy-start(f32[2048,32]{0,1:T(8,128)S(1)} %get-tuple-element.429) | copy-start | bytes 786436
  263.1 6.7 copy-start.4
  269.8 1.1 copy-start.14
  269.8 143.2 %copy-start.2 = (bf16[512,1024]{1,0:T(8,128)(2,1)S(1)}, bf16[512,1024]{1,0:T(8,128)(2,1)}, u32[]{:S(2)}) copy-start(bf16[512,1024]{1,0:T(8,128)(2,1)} %param.17) | copy-start | bytes 3145732
  269.8 248.2 %all-gather.13.cloned.1.call-start = ((), (), s32[]{:S(2)}) async-start(), calls=%async_computation.13 | async-start | bytes 3244032 | tf_op jit(solution)/shard_map/all_gather | solution.py:137
  271.7 143.3 %copy-start.17 = (f32[1,1024]{1,0:T(1,128)S(1)}, f32[1,1024]{1,0:T(1,128)}, u32[]{:S(2)}) copy-start(f32[1,1024]{1,0:T(1,128)} %get-tuple-element.425) | copy-start | bytes 12292
  271.7 284.7 %all-gather.11.cloned.1.call-start = ((), (), s32[]{:S(2)}) async-start(), calls=%async_computation.12 | async-start | bytes 5242880 | tf_op jit(solution)/shard_map/all_gather | solution.py:168
  414.9 339.5 %copy-start = (f32[512,1024]{1,0:T(8,128)}, f32[512,1024]{1,0:T(8,128)S(1)}, u32[]{:S(2)}) copy-start(f32[512,1024]{1,0:T(8,128)S(1)} %get-tuple-element.395) | copy-start | bytes 6291460
  414.9 2.0 copy-start.6
  414.9 6.4 copy-start.15
  415.0 339.4 %copy-start.21 = (f32[512]{0:T(512)}, f32[512]{0:T(512)S(1)}, u32[]{:S(2)}) copy-start(f32[512]{0:T(512)S(1)} %add_rsqrt_fusion) | copy-start | bytes 6148
  416.2 167.7 %all-gather.15.cloned.1.call-start = ((), (), s32[]{:S(2)}) async-start(), calls=%async_computation.14 | async-start | bytes 1622016 | tf_op jit(solution)/shard_map/all_gather | solution.py:138
  416.9 28.0 %collective-permute-start = (bf16[512,1024]{1,0:T(8,128)(2,1)S(1)}, bf16[512,1024]{1,0:T(8,128)(2,1)}, u32[]{:S(2)}, u32[]{:S(2)}) collective-permute-start(bf16[512,1024]{1,0:T(8,128)(2,1)S(1)} %copy-done.6), channel_id=1, source_target_pairs={{0,1},{1,2},{2,3},{3,0},{4,5},{5,6},{6,7},{7,4},{8,9},{9,10},{10,1... | collective-permute-start | bytes 3145736 | tf_op jit(solution)/shard_map/ppermute | solution.py:214
  418.1 61.4 %collective-permute-start.1 = (bf16[512,1024]{1,0:T(8,128)(2,1)S(1)}, bf16[512,1024]{1,0:T(8,128)(2,1)}, u32[]{:S(2)}, u32[]{:S(2)}) collective-permute-start(bf16[512,1024]{1,0:T(8,128)(2,1)S(1)} %copy-done.6), channel_id=1, source_target_pairs={{0,3},{1,0},{2,1},{3,2},{4,7},{5,4},{6,5},{7,6},{8,11},{9,8},{10,9... | collective-permute-start | bytes 3145736 | tf_op jit(solution)/shard_map/ppermute | solution.py:219
  422.0 329.4 %reduce-scatter.16.cloned.1.call-start = ((), (), s32[]{:S(2)}) async-start(), calls=%async_computation.16 | async-start | bytes 10485760 | tf_op jit(solution)/shard_map/reduce_scatter | solution.py:231
  445.0 70.8 %collective-permute-start.2 = (bf16[512,1024]{1,0:T(8,128)(2,1)}, bf16[512,1024]{1,0:T(8,128)(2,1)}, u32[]{:S(2)}, u32[]{:S(2)}) collective-permute-start(bf16[512,1024]{1,0:T(8,128)(2,1)} %collective-permute-done), channel_id=1, source_target_pairs={{0,1},{1,2},{2,3},{3,0},{4,5},{5,6},{6,7},{7,4},{8,9},{9,10},{10,1... | collective-permute-start | bytes 3145736 | tf_op jit(solution)/shard_map/ppermute | solution.py:214
  583.9 13.9 copy-start.28
  595.3 1.5 copy-start.30
  595.3 2.6 copy-start.31
  606.8 230.8 %all-gather.17.cloned.1.call-start = ((), (), s32[]{:S(2)}) async-start(), calls=%async_computation.17 | async-start | bytes 5242880 | tf_op jit(solution)/shard_map/all_gather | solution.py:242
  751.5 2.9 copy-start.5
  754.4 1.6 copy-start.25
  756.0 335.5 %reduce-scatter.18.cloned.1.call-start = ((), (), s32[]{:S(2)}) async-start(), calls=%async_computation.18 | async-start | bytes 5242880 | tf_op jit(solution)/shard_map/reduce_scatter | solution.py:260
  843.1 155.5 %copy-start.8 = (f32[2048,32]{0,1:T(8,128)S(1)}, f32[2048,32]{0,1:T(8,128)}, u32[]{:S(2)}) copy-start(f32[2048,32]{0,1:T(8,128)} %copy-done.7) | copy-start | bytes 786436
  1002.6 3.9 copy-start.9
  1016.1 1.2 copy-start.12
  1016.1 1.5 copy-start.13
  1016.2 125.9 %reduce-scatter.20.cloned.1.call-start = ((), (), s32[]{:S(2)}) async-start(), calls=%async_computation.19 | async-start | bytes 3538944 | tf_op jit(solution)/shard_map/reduce_scatter | solution.py:274
  1025.1 1.4 copy-start.29
  1025.1 196.0 %reduce-scatter.14.cloned.1.call-start = ((), (), s32[]{:S(2)}) async-start(), calls=%async_computation.15 | async-start | bytes 5242880 | tf_op jit(solution)/shard_map/reduce_scatter | solution.py:176
  1033.4 58.2 %copy-start.3 = (bf16[512,1024]{1,0:T(8,128)(2,1)S(1)}, bf16[512,1024]{1,0:T(8,128)(2,1)}, u32[]{:S(2)}) copy-start(bf16[512,1024]{1,0:T(8,128)(2,1)} %param.17) | copy-start | bytes 3145732
  1033.4 58.2 %copy-start.20 = (f32[1,1024]{1,0:T(1,128)S(1)}, f32[1,1024]{1,0:T(1,128)}, u32[]{:S(2)}) copy-start(f32[1,1024]{1,0:T(1,128)} %copy-done.19) | copy-start | bytes 12292
  1033.4 58.2 %copy-start.24 = (f32[512]{0:T(512)S(1)}, f32[512]{0:T(512)}, u32[]{:S(2)}) copy-start(f32[512]{0:T(512)} %copy-done.23) | copy-start | bytes 6148
  1033.4 60.2 %copy-start.27 = (f32[1024]{0:T(1024)S(1)}, f32[1024]{0:T(1024)}, u32[]{:S(2)}) copy-start(f32[1024]{0:T(1024)} %get-tuple-element.318) | copy-start | bytes 12292
  1033.4 225.6 %reduce-scatter.28.cloned.1.call-start = ((), (), s32[]{:S(2)}) async-start(), calls=%async_computation.23 | async-start | bytes 589824
  1094.7 213.1 %reduce-scatter.26.cloned.1.call-start = ((), (), s32[]{:S(2)}) async-start(), calls=%async_computation.22 | async-start | bytes 3244032 | tf_op jit(solution)/shard_map/reduce_scatter | solution.py:277
  1102.6 268.7 %reduce-scatter.24.cloned.1.call-start = ((), (), s32[]{:S(2)}) async-start(), calls=%async_computation.21 | async-start | bytes 6488064 | tf_op jit(solution)/shard_map/reduce_scatter | solution.py:276
  1114.1 1.2 copy-start.10
  1114.2 296.7 %reduce-scatter.22.cloned.1.call-start = ((), (), s32[]{:S(2)}) async-start(), calls=%async_computation.20 | async-start | bytes 1179648 | tf_op jit(solution)/shard_map/reduce_scatter | solution.py:275
  1119.8 101.3 %copy-start.1 = (f32[512,1024]{1,0:T(8,128)S(1)}, f32[512,1024]{1,0:T(8,128)}, u32[]{:S(2)}) copy-start(f32[512,1024]{1,0:T(8,128)} %copy-done) | copy-start | bytes 6291460
  1119.9 101.3 %copy-start.18 = (f32[1,1024]{1,0:T(1,128)S(1)}, f32[1,1024]{1,0:T(1,128)}, u32[]{:S(2)}) copy-start(f32[1,1024]{1,0:T(1,128)} %get-tuple-element.425) | copy-start | bytes 12292
  1119.9 101.3 %copy-start.22 = (f32[512]{0:T(512)S(1)}, f32[512]{0:T(512)}, u32[]{:S(2)}) copy-start(f32[512]{0:T(512)} %copy-done.21) | copy-start | bytes 6148
  1119.9 101.3 %copy-start.26 = (f32[512]{0:T(512)S(1)}, f32[512]{0:T(512)}, u32[]{:S(2)}) copy-start(f32[512]{0:T(512)} %copy-done.25) | copy-start | bytes 6148
Sparse Core Ops, SparseCore 0:
  10.5 30.0 all-gather.8
  42.7 80.7 all-gather.6
  270.0 142.9 reduce-scatter.11
  415.3 32.3 all-gather.12
  449.7 106.7 all-gather.10
  558.8 25.1 all-gather.14
  607.0 144.4 reduce-scatter.15
  756.2 81.4 all-gather.16
  1016.3 75.2 reduce-scatter.17
  1095.2 46.7 reduce-scatter.19
  1144.3 76.7 reduce-scatter.13
  1224.3 34.6 reduce-scatter.27
  1263.0 44.8 reduce-scatter.25
  1312.2 59.0 reduce-scatter.23
  1374.8 35.9 reduce-scatter.21
